TPU v7x, 512 devices: a whole 4x8x8 slice. The times are simulated.
512 devices in a mesh: node: 64 (over y, z), col: 8 (over x, core).
Axes of the slice: x: 4, y: 8, z: 8, core: 2. Of those that a mesh axis runs over, the one named last changes fastest.
Arguments:
- x_t: bfloat16 [512, 32768], P('col', 'node'), may hold values from -6 to 6
- adj_tiles: bfloat16 [4096, 128, 128], P('node'), may hold values from -0.1875 to 0.1875
- tile_rows: int32 [4096], P('node'), may hold values from 0 to 3
- tile_cols: int32 [4096], P('node'), may hold values from 0 to 255, as said below
- tile_counts: int32 [64], P('node'), may hold values from 8 to 64, as said below
- w_first: bfloat16 [512, 512], P('col'), may hold values from -0.25 to 0.25
- b_first: float32 [512], P('col'), may hold values from -3 to 3
- w_second: bfloat16 [512, 512], P('col'), may hold values from -0.25 to 0.25
- b_second: float32 [512], P('col'), may hold values from -3 to 3
Outputs:
- out_t: float32 [512, 32768], P('col', 'node')
Inputs may be any that keep to these rules, and one draw needn't show every extreme that they name: `tile_cols`: column blocks q * 4 to q * 4 + 3 belong to device q of node. Among the live tiles of one device, at most 2 distinct column blocks belong to any one device, and every device's first 2 tiles name 2 distinct blocks of one device. `tile_counts`: some device has all 64 slots live.
All inputs are finite; a program needn't handle non-finite values.
Results may differ from a plain program's by a relative error of at most 0.004.
Values may be sent and summed in bfloat16 or wider, within the bound.
A program may use at most 64 MiB of HBM per device.

v0:
```python
import jax
import jax.numpy as jnp
from jax import lax
from jax.sharding import PartitionSpec as P

BLK = 128
CAP = 2


def tile_sum(x_blocks, tile_values, selector):
    products = jnp.einsum("fnj,nij->fni", x_blocks, tile_values, preferred_element_type=jnp.float32)
    return jnp.einsum("fni,nb->fbi", products, selector, precision=lax.Precision.HIGHEST)


def aggregate(feat_t, adj_tiles, tile_rows, live_count, plan):
    feat_local = feat_t.shape[0]
    row_blocks = feat_t.shape[1] // BLK
    tile_total = adj_tiles.shape[0]
    asked_of, tile_slot = plan
    own_blocks = feat_t.reshape(feat_local, row_blocks, BLK)
    outgoing = jnp.take(own_blocks, asked_of.reshape(-1), axis=1)
    incoming = lax.all_to_all(outgoing, "node", split_axis=1, concat_axis=1, tiled=True)
    x_blocks = jnp.take(incoming, tile_slot, axis=1)
    is_live = jnp.arange(tile_total, dtype=jnp.int32) < live_count
    selector = (
        (tile_rows[:, None] == jnp.arange(row_blocks, dtype=jnp.int32)[None, :]) & is_live[:, None]
    ).astype(jnp.float32)
    summed = tile_sum(x_blocks, adj_tiles, selector)
    return summed.reshape(feat_local, row_blocks * BLK).astype(jnp.bfloat16)


def dense_layer(aggregated, weight_local, bias_local):
    summed = jnp.dot(
        weight_local,
        lax.all_gather(aggregated, "col", axis=0, tiled=True),
        preferred_element_type=jnp.float32,
    )
    return summed + bias_local[:, None]


def body(x_t, adj_tiles, tile_rows, tile_cols, tile_counts, w_first, b_first, w_second, b_second):
    row_blocks = x_t.shape[1] // BLK
    peer_count = lax.axis_size("node")
    block_total = peer_count * row_blocks
    live_count = tile_counts[0]
    is_live = jnp.arange(tile_cols.shape[0], dtype=jnp.int32) < live_count
    named = (tile_cols[:, None] == jnp.arange(block_total, dtype=jnp.int32)[None, :]) & is_live[
        :, None
    ]
    needed = jnp.any(named, axis=0).astype(jnp.int32).reshape(peer_count, row_blocks)
    position = jnp.cumsum(needed, axis=1) - 1
    slot_hit = (needed[:, :, None] == 1) & (
        position[:, :, None] == jnp.arange(CAP, dtype=jnp.int32)[None, None, :]
    )
    wanted = jnp.sum(
        slot_hit.astype(jnp.int32) * jnp.arange(row_blocks, dtype=jnp.int32)[None, :, None], axis=1
    )
    asked_of = lax.all_to_all(wanted, "node", split_axis=0, concat_axis=0, tiled=True)
    owner_base = (jnp.arange(peer_count, dtype=jnp.int32) * CAP)[:, None]
    slot_table = (owner_base + jnp.clip(position, 0, CAP - 1)).reshape(-1)
    tile_slot = jnp.take(slot_table, tile_cols)
    plan = (asked_of, tile_slot)
    y_first = aggregate(x_t, adj_tiles, tile_rows, live_count, plan)
    h_first = jnp.maximum(dense_layer(y_first, w_first, b_first), 0.0).astype(jnp.bfloat16)
    y_second = aggregate(h_first, adj_tiles, tile_rows, live_count, plan)
    return dense_layer(y_second, w_second, b_second)


def solution(mesh):
    return jax.shard_map(
        body,
        mesh=mesh,
        in_specs=(
            P("col", "node"),
            P("node", None, None),
            P("node"),
            P("node"),
            P("node"),
            P("col", None),
            P("col"),
            P("col", None),
            P("col"),
        ),
        out_specs=P("col", "node"),
        check_vma=False,
    )
```

profile of v0, /device:TPU:25, one launch (start us, length us, event | category | flops | bytes accessed | tf_op | source)
XLA Modules:
  0.0 206.9 jit_solution(1067784979185888805)
XLA Ops:
  0.8 0.8 fusion.23
  1.6 0.1 reshape.72
  1.7 0.1 copy.23
  1.8 0.2 reduce_window_sum.11
  2.0 0.1 clamp_add_fusion
  2.1 0.1 copy.24
  2.2 0.7 copy.25
  2.9 15.8 %all-to-all-start = ((s32[64,1,2]{2,1,0:T(1,128)}), s32[64,1,2]{2,1,0:T(1,128)S(1)}, u32[]{:S(2)}, u32[]{:S(2)}) async-start(s32[64,1,2]{2,1,0:T(1,128)} %copy.25), calls=%async_computation | async-start | bytes 65536 | tf_op jit(solution)/shard_map/all_to_all | solution.py:58
  18.7 0.9 copy_bitcast_fusion.3
  19.6 7.5 %all-to-all-done = s32[64,1,2]{2,1,0:T(1,128)S(1)} async-done(((s32[64,1,2]{2,1,0:T(1,128)}), s32[64,1,2]{2,1,0:T(1,128)S(1)}, u32[]{:S(2)}, u32[]{:S(2)}) %all-to-all-start) | async-done | bytes 544 | tf_op jit(solution)/shard_map/all_to_all | solution.py:58
  27.1 0.5 broadcast.114
  27.6 0.7 reduce.3
  28.3 0.1 reshape.70
  28.5 2.1 %gather_fusion.1 = bf16[128,64,128]{2,1,0:T(8,128)(2,1)} fusion(bf16[64,4,128]{2,0,1:T(8,128)(2,1)S(1)} %copy_bitcast_fusion.3, s32[1024]{0:T(1024)S(1)} %pad_clamp_fusion.1), kind=kCustom, calls=%fused_computation.clone | custom fusion | bytes 4194816 | tf_op jit(solution)/shard_map/jit(_take)/gather | solution.py:21
  30.6 3.2 %select_bitcast_fusion.1 = bf16[64,128,128]{2,0,1:T(8,128)(2,1)} fusion(bf16[128,64,128]{2,1,0:T(8,128)(2,1)} %gather_fusion.1, pred[128]{0:T(512)(128)(4,1)S(1)} %compare_and_fusion.1), kind=kLoop, calls=%fused_computation.10 | loop fusion | flops 1048576 | bytes 4194432 | tf_op jit(solution)/shard_map/jit(_take)/select_n | solution.py:21
  33.8 8.0 %all-to-all-start.1 = ((bf16[64,128,128]{2,0,1:T(8,128)(2,1)}), bf16[64,128,128]{2,0,1:T(8,128)(2,1)}, u32[]{:S(2)}, u32[]{:S(2)}) async-start(bf16[64,128,128]{2,0,1:T(8,128)(2,1)} %select_bitcast_fusion.1), calls=%async_computation.1 | async-start | bytes 4194304 | tf_op jit(solution)/shard_map/all_to_all | solution.py:22
  41.8 0.1 add.63
  42.0 0.8 gather_fusion
  42.8 53.7 %all-to-all-done.1 = bf16[64,128,128]{2,0,1:T(8,128)(2,1)} async-done(((bf16[64,128,128]{2,0,1:T(8,128)(2,1)}), bf16[64,128,128]{2,0,1:T(8,128)(2,1)}, u32[]{:S(2)}, u32[]{:S(2)}) %all-to-all-start.1) | async-done | bytes 2097184 | tf_op jit(solution)/shard_map/all_to_all | solution.py:22
  96.5 2.3 %gather_fusion.2 = bf16[64,64,128]{2,1,0:T(8,128)(2,1)S(1)} fusion(bf16[64,128,128]{2,0,1:T(8,128)(2,1)} %all-to-all-done.1, s32[1024]{0:T(1024)S(1)} %pad_clamp_fusion), kind=kCustom, calls=%fused_computation.1.clone | custom fusion | bytes 2097408 | tf_op jit(solution)/shard_map/jit(_take)/gather | solution.py:23
  98.8 1.5 convolution_bitcast_fusion.1
  100.4 2.0 fusion.7
  102.4 15.1 %all_gather.6 = bf16[512,512]{1,0:T(8,128)(2,1)S(1)} all-gather(bf16[64,512]{1,0:T(8,128)(2,1)S(1)} %bitcast.53), channel_id=1, replica_groups=mesh['node'=64,'col'=8] {'col'}, dimensions={0}, use_global_device_ids=true | all-gather | bytes 589824 | tf_op jit(solution)/shard_map/all_gather | solution.py:35
  117.5 0.2 fusion.13
  117.7 2.2 %gather_fusion.3 = bf16[128,64,128]{2,1,0:T(8,128)(2,1)} fusion(bf16[64,4,128]{2,0,1:T(8,128)(2,1)S(1)} %bitcast.50, s32[1024]{0:T(1024)S(1)} %pad_clamp_fusion.1), kind=kCustom, calls=%fused_computation.2.clone | custom fusion | bytes 4194816 | tf_op jit(solution)/shard_map/jit(_take)/gather | solution.py:21
  119.9 1.9 select_bitcast_fusion
  121.7 62.4 %all_to_all.19 = bf16[64,128,128]{2,0,1:T(8,128)(2,1)} all-to-all(bf16[64,128,128]{2,0,1:T(8,128)(2,1)S(1)} %select_bitcast_fusion), channel_id=1, replica_groups=mesh['node'=64,'col'=8] {'node'}, dimensions={1} | all-to-all | bytes 4194304 | tf_op jit(solution)/shard_map/all_to_all | solution.py:22
  184.1 2.3 %gather_fusion.4 = bf16[64,64,128]{2,1,0:T(8,128)(2,1)S(1)} fusion(bf16[64,128,128]{2,0,1:T(8,128)(2,1)} %all_to_all.19, s32[1024]{0:T(1024)S(1)} %pad_clamp_fusion), kind=kCustom, calls=%fused_computation.3.clone | custom fusion | bytes 2097408 | tf_op jit(solution)/shard_map/jit(_take)/gather | solution.py:23
  186.4 1.5 convolution_bitcast_fusion
  188.0 2.0 fusion.10
  190.0 16.0 %all_gather.7 = bf16[512,512]{1,0:T(8,128)(2,1)S(1)} all-gather(bf16[64,512]{1,0:T(8,128)(2,1)S(1)} %bitcast.54), channel_id=1, replica_groups=mesh['node'=64,'col'=8] {'col'}, dimensions={0}, use_global_device_ids=true | all-gather | bytes 589824 | tf_op jit(solution)/shard_map/all_gather | solution.py:35
  206.0 0.9 fusion.4
  (29 shorter events, 0.2 us)
Async XLA Ops:
  0.0 98.8 %copy-start = (bf16[64,128,128]{2,1,0:T(8,128)(2,1)S(1)}, bf16[64,128,128]{2,1,0:T(8,128)(2,1)}, u32[]{:S(2)}) copy-start(bf16[64,128,128]{2,1,0:T(8,128)(2,1)} %param.14) | copy-start | bytes 6291460
  2.9 24.2 %all-to-all-start = ((s32[64,1,2]{2,1,0:T(1,128)}), s32[64,1,2]{2,1,0:T(1,128)S(1)}, u32[]{:S(2)}, u32[]{:S(2)}) async-start(s32[64,1,2]{2,1,0:T(1,128)} %copy.25), calls=%async_computation | async-start | bytes 65536 | tf_op jit(solution)/shard_map/all_to_all | solution.py:58
  33.8 8.1 %copy-start.5 = (s32[64]{0:T(128)S(1)}, s32[64]{0:T(128)}, u32[]{:S(2)}) copy-start(s32[64]{0:T(128)} %param.16) | copy-start | bytes 772
  33.8 62.7 %all-to-all-start.1 = ((bf16[64,128,128]{2,0,1:T(8,128)(2,1)}), bf16[64,128,128]{2,0,1:T(8,128)(2,1)}, u32[]{:S(2)}, u32[]{:S(2)}) async-start(bf16[64,128,128]{2,0,1:T(8,128)(2,1)} %select_bitcast_fusion.1), calls=%async_computation.1 | async-start | bytes 4194304 | tf_op jit(solution)/shard_map/all_to_all | solution.py:22
  98.8 1.6 copy-start.3
  100.4 17.1 %copy-start.1 = (bf16[64,512]{1,0:T(8,128)(2,1)S(1)}, bf16[64,512]{1,0:T(8,128)(2,1)}, u32[]{:S(2)}) copy-start(bf16[64,512]{1,0:T(8,128)(2,1)} %param.18) | copy-start | bytes 196612
  100.4 17.1 %copy-start.6 = (f32[64]{0:T(128)S(1)}, f32[64]{0:T(128)}, u32[]{:S(2)}) copy-start(f32[64]{0:T(128)} %param.19) | copy-start | bytes 772
  188.0 18.1 %copy-start.2 = (bf16[64,512]{1,0:T(8,128)(2,1)S(1)}, bf16[64,512]{1,0:T(8,128)(2,1)}, u32[]{:S(2)}) copy-start(bf16[64,512]{1,0:T(8,128)(2,1)} %param.20) | copy-start | bytes 196612
  188.0 18.0 %copy-start.4 = (f32[64]{0:T(128)S(1)}, f32[64]{0:T(128)}, u32[]{:S(2)}) copy-start(f32[64]{0:T(128)} %param.21) | copy-start | bytes 772
where the time goes:
time: 207 us
  blocking collectives  93.5 us (45%)
  waiting for transfers between devices  61.2 us (30%)
  starting transfers between devices  23.9 us (12%)
  local copies, waits for them, and re-layouts  12.4 us (6%)
  matrix products  8.07 us (4%)
  other arithmetic  6.84 us (3%)
    all_to_all x1, blocking collectives, aggregate(): lax.all_to_all(outgoing, 'node', split_axis=1, concat_axis=1, tiled=True)  62.4 us
    all_to_all x1, waiting for transfers between devices, aggregate(): lax.all_to_all(outgoing, 'node', split_axis=1, concat_axis=1, tiled=True)  53.7 us
    all_gather x2, blocking collectives, dense_layer(): lax.all_gather(aggregated, 'col', axis=0, tiled=True)  31.1 us
    all_to_all x1, starting transfers between devices, body(): lax.all_to_all(wanted, 'node', split_axis=0, concat_axis=0, tiled=True)  15.8 us
    all_to_all x1, starting transfers between devices, aggregate(): lax.all_to_all(outgoing, 'node', split_axis=1, concat_axis=1, tiled=True)  8.02 us
    all_to_all x1, waiting for transfers between devices, body(): lax.all_to_all(wanted, 'node', split_axis=0, concat_axis=0, tiled=True)  7.51 us
    select_n x3, other arithmetic, aggregate(): outgoing = jnp.take(own_blocks, asked_of.reshape(-1), axis=1)  5.01 us
    gather x2, local copies, waits for them, and re-layouts, aggregate(): x_blocks = jnp.take(incoming, tile_slot, axis=1)  4.68 us
  transfers between devices with their start and end apart: 2, of which 2 were waited for; matrix products, arithmetic and copies ran while one was open for 1% of the time, Pallas kernels for 0%

commit v1 on v0

--- a/solution.py
+++ b/solution.py
@@ -5,6 +5,24 @@
 
 BLK = 128
 CAP = 2
+
+
+def collect(value, axis, dim):
+    ways, here, step = (lax.axis_size(axis), lax.axis_index(axis), value.shape[dim])
+    shape = [n * ways if d == dim else n for d, n in enumerate(value.shape)]
+    full = lax.dynamic_update_slice_in_dim(
+        jnp.zeros(shape, value.dtype), value, here * step, axis=dim
+    )
+    going_up = going_down = value
+    for far in range(1, ways // 2 + 1):
+        going_up = lax.ppermute(going_up, axis, [(d, (d + 1) % ways) for d in range(ways)])
+        full = lax.dynamic_update_slice_in_dim(full, going_up, (here - far) % ways * step, axis=dim)
+        if 2 * far < ways:
+            going_down = lax.ppermute(going_down, axis, [(d, (d - 1) % ways) for d in range(ways)])
+            full = lax.dynamic_update_slice_in_dim(
+                full, going_down, (here + far) % ways * step, axis=dim
+            )
+    return full
 
 
 def tile_sum(x_blocks, tile_values, selector):
@@ -31,9 +49,7 @@
 
 def dense_layer(aggregated, weight_local, bias_local):
     summed = jnp.dot(
-        weight_local,
-        lax.all_gather(aggregated, "col", axis=0, tiled=True),
-        preferred_element_type=jnp.float32,
+        weight_local, collect(aggregated, "col", 0), preferred_element_type=jnp.float32
     )
     return summed + bias_local[:, None]
 

time: 207 us -> 215 us (1.039); the launches traced: 207 us -> 211 us
  blocking collectives: 93.5 us -> 59.9 us
  starting transfers between devices: 23.9 us -> 47.8 us
  waiting for transfers between devices: 61.2 us -> 74.7 us
    all_gather x2 -> x0, blocking collectives: 31.1 us -> none  [dense_layer(): lax.all_gather(aggregated, 'col', axis=0, tiled=True)]
    ppermute x0 -> x14, starting transfers between devices: none -> 24 us  [the longest x8 15.8 us: collect(): lax.ppermute(going_up, axis, [(d, (d + 1) % ways) for d in range(ways)])]
    ppermute x0 -> x14, waiting for transfers between devices: none -> 13.7 us  [the longest x8 12.9 us: collect(): lax.ppermute(going_up, axis, [(d, (d + 1) % ways) for d in range(ways)])]
    all_to_all x1, blocking collectives: 62.4 us -> 59.9 us  [aggregate(): lax.all_to_all(outgoing, 'node', split_axis=1, concat_axis=1, tiled=True)]
  transfers between devices with their start and end apart: 2 -> 16, of which waited for: 2 -> 13; matrix products, arithmetic and copies ran while one was open for 1% -> 1% of each run, Pallas kernels for 0% -> 0%
where the time goes in v1:
time: 215 us; the launch traced here: 211 us
  waiting for transfers between devices  74.7 us (35%)
  blocking collectives  59.9 us (28%)
  starting transfers between devices  47.8 us (22%)
  local copies, waits for them, and re-layouts  12.6 us (6%)
  matrix products  8.07 us (4%)
  other arithmetic  6.85 us (3%)
    all_to_all x1, blocking collectives, aggregate(): lax.all_to_all(outgoing, 'node', split_axis=1, concat_axis=1, tiled=True)  59.9 us
    all_to_all x1, waiting for transfers between devices, aggregate(): lax.all_to_all(outgoing, 'node', split_axis=1, concat_axis=1, tiled=True)  53.5 us
    all_to_all x1, starting transfers between devices, body(): lax.all_to_all(wanted, 'node', split_axis=0, concat_axis=0, tiled=True)  15.8 us
    ppermute x8, starting transfers between devices, collect(): lax.ppermute(going_up, axis, [(d, (d + 1) % ways) for d in range(ways)])  15.8 us
    ppermute x8, waiting for transfers between devices, collect(): lax.ppermute(going_up, axis, [(d, (d + 1) % ways) for d in range(ways)])  12.9 us
    ppermute x6, starting transfers between devices, collect(): lax.ppermute(going_down, axis, [(d, (d - 1) % ways) for d in range(ways)])  8.18 us
    all_to_all x1, starting transfers between devices, aggregate(): lax.all_to_all(outgoing, 'node', split_axis=1, concat_axis=1, tiled=True)  8.01 us
    all_to_all x1, waiting for transfers between devices, body(): lax.all_to_all(wanted, 'node', split_axis=0, concat_axis=0, tiled=True)  7.51 us
  transfers between devices with their start and end apart: 16, of which 13 were waited for; matrix products, arithmetic and copies ran while one was open for 1% of the time, Pallas kernels for 0%

profile of v1, /device:TPU:25, one launch (start us, length us, event | category | flops | bytes accessed | tf_op | source)
XLA Modules:
  0.0 211.3 jit_solution(11272574395846269757)
XLA Ops:
  2.9 15.8 %all-to-all-start = ((s32[64,1,2]{2,1,0:T(1,128)}), s32[64,1,2]{2,1,0:T(1,128)S(1)}, u32[]{:S(2)}, u32[]{:S(2)}) async-start(s32[64,1,2]{2,1,0:T(1,128)} %copy.25), calls=%async_computation | async-start | bytes 65536 | tf_op jit(solution)/shard_map/all_to_all | solution.py:74
  18.7 0.9 copy_bitcast_fusion.3
  19.6 7.5 %all-to-all-done = s32[64,1,2]{2,1,0:T(1,128)S(1)} async-done(((s32[64,1,2]{2,1,0:T(1,128)}), s32[64,1,2]{2,1,0:T(1,128)S(1)}, u32[]{:S(2)}, u32[]{:S(2)}) %all-to-all-start) | async-done | bytes 544 | tf_op jit(solution)/shard_map/all_to_all | solution.py:74
  28.5 2.1 %gather_fusion.1 = bf16[128,64,128]{2,1,0:T(8,128)(2,1)} fusion(bf16[64,4,128]{2,0,1:T(8,128)(2,1)S(1)} %copy_bitcast_fusion.3, s32[1024]{0:T(1024)S(1)} %pad_clamp_fusion.1), kind=kCustom, calls=%fused_computation.clone | custom fusion | bytes 4194816 | tf_op jit(solution)/shard_map/jit(_take)/gather | solution.py:39
  30.7 3.2 %select_bitcast_fusion.1 = bf16[64,128,128]{2,0,1:T(8,128)(2,1)} fusion(bf16[128,64,128]{2,1,0:T(8,128)(2,1)} %gather_fusion.1, pred[128]{0:T(512)(128)(4,1)S(1)} %compare_and_fusion.1), kind=kLoop, calls=%fused_computation.10 | loop fusion | flops 1048576 | bytes 4194432 | tf_op jit(solution)/shard_map/jit(_take)/select_n | solution.py:39
  33.8 8.0 %all-to-all-start.1 = ((bf16[64,128,128]{2,0,1:T(8,128)(2,1)}), bf16[64,128,128]{2,0,1:T(8,128)(2,1)}, u32[]{:S(2)}, u32[]{:S(2)}) async-start(bf16[64,128,128]{2,0,1:T(8,128)(2,1)} %select_bitcast_fusion.1), calls=%async_computation.1 | async-start | bytes 4194304 | tf_op jit(solution)/shard_map/all_to_all | solution.py:40
  42.1 0.8 gather_fusion
  43.0 53.5 %all-to-all-done.1 = bf16[64,128,128]{2,0,1:T(8,128)(2,1)} async-done(((bf16[64,128,128]{2,0,1:T(8,128)(2,1)}), bf16[64,128,128]{2,0,1:T(8,128)(2,1)}, u32[]{:S(2)}, u32[]{:S(2)}) %all-to-all-start.1) | async-done | bytes 2097184 | tf_op jit(solution)/shard_map/all_to_all | solution.py:40
  96.5 2.3 %gather_fusion.2 = bf16[64,64,128]{2,1,0:T(8,128)(2,1)S(1)} fusion(bf16[64,128,128]{2,0,1:T(8,128)(2,1)} %all-to-all-done.1, s32[1024]{0:T(1024)S(1)} %pad_clamp_fusion), kind=kCustom, calls=%fused_computation.1.clone | custom fusion | bytes 2097408 | tf_op jit(solution)/shard_map/jit(_take)/gather | solution.py:41
  98.9 1.5 convolution_bitcast_fusion.1
  100.4 2.0 fusion.7
  102.4 2.9 %collective-permute-start = (bf16[64,512]{1,0:T(8,128)(2,1)S(1)}, bf16[64,512]{1,0:T(8,128)(2,1)S(1)}, u32[]{:S(2)}, u32[]{:S(2)}) collective-permute-start(bf16[64,512]{1,0:T(8,128)(2,1)S(1)} %bitcast.61), channel_id=1, source_target_pairs={{0,1},{1,2},{2,3},{3,4},{4,5},{5,6},{6,7},{7,0},{8,9},{9,10},{10,1... | collective-permute-start | bytes 196616 | tf_op jit(solution)/shard_map/ppermute | solution.py:18
  105.4 1.3 collective-permute-done
  106.6 2.4 %collective-permute-start.2 = (bf16[64,512]{1,0:T(8,128)(2,1)S(1)}, bf16[64,512]{1,0:T(8,128)(2,1)S(1)}, u32[]{:S(2)}, u32[]{:S(2)}) collective-permute-start(bf16[64,512]{1,0:T(8,128)(2,1)S(1)} %collective-permute-done), channel_id=1, source_target_pairs={{0,1},{1,2},{2,3},{3,4},{4,5},{5,6},{6,7},{7,0},{8,9},{9,10},{10,1... | collective-permute-start | bytes 196616 | tf_op jit(solution)/shard_map/ppermute | solution.py:18
  109.2 1.2 collective-permute-done.2
  110.3 2.4 %collective-permute-start.4 = (bf16[64,512]{1,0:T(8,128)(2,1)S(1)}, bf16[64,512]{1,0:T(8,128)(2,1)S(1)}, u32[]{:S(2)}, u32[]{:S(2)}) collective-permute-start(bf16[64,512]{1,0:T(8,128)(2,1)S(1)} %collective-permute-done.2), channel_id=1, source_target_pairs={{0,1},{1,2},{2,3},{3,4},{4,5},{5,6},{6,7},{7,0},{8,9},{9,10},{10,1... | collective-permute-start | bytes 196616 | tf_op jit(solution)/shard_map/ppermute | solution.py:18
  113.0 1.0 collective-permute-start.5
  114.8 1.6 collective-permute-start.6
  116.7 3.0 %collective-permute-done.6 = bf16[64,512]{1,0:T(8,128)(2,1)S(1)} collective-permute-done((bf16[64,512]{1,0:T(8,128)(2,1)S(1)}, bf16[64,512]{1,0:T(8,128)(2,1)S(1)}, u32[]{:S(2)}, u32[]{:S(2)}) %collective-permute-start.6) | collective-permute-done | bytes 65568 | tf_op jit(solution)/shard_map/ppermute | solution.py:18
  119.9 2.1 %gather_fusion.3 = bf16[128,64,128]{2,1,0:T(8,128)(2,1)} fusion(bf16[64,4,128]{2,0,1:T(8,128)(2,1)S(1)} %bitcast.54, s32[1024]{0:T(1024)S(1)} %pad_clamp_fusion.1), kind=kCustom, calls=%fused_computation.2.clone | custom fusion | bytes 4194816 | tf_op jit(solution)/shard_map/jit(_take)/gather | solution.py:39
  122.1 1.9 select_bitcast_fusion
  123.9 59.9 %all_to_all.19 = bf16[64,128,128]{2,0,1:T(8,128)(2,1)} all-to-all(bf16[64,128,128]{2,0,1:T(8,128)(2,1)S(1)} %select_bitcast_fusion), channel_id=1, replica_groups=mesh['node'=64,'col'=8] {'node'}, dimensions={1} | all-to-all | bytes 4194304 | tf_op jit(solution)/shard_map/all_to_all | solution.py:40
  183.8 2.3 %gather_fusion.4 = bf16[64,64,128]{2,1,0:T(8,128)(2,1)S(1)} fusion(bf16[64,128,128]{2,0,1:T(8,128)(2,1)} %all_to_all.19, s32[1024]{0:T(1024)S(1)} %pad_clamp_fusion), kind=kCustom, calls=%fused_computation.3.clone | custom fusion | bytes 2097408 | tf_op jit(solution)/shard_map/jit(_take)/gather | solution.py:41
  186.2 1.5 convolution_bitcast_fusion
  187.8 2.0 fusion.10
  189.7 4.1 %collective-permute-start.7 = (bf16[64,512]{1,0:T(8,128)(2,1)S(1)}, bf16[64,512]{1,0:T(8,128)(2,1)S(1)}, u32[]{:S(2)}, u32[]{:S(2)}) collective-permute-start(bf16[64,512]{1,0:T(8,128)(2,1)S(1)} %bitcast.59), channel_id=1, source_target_pairs={{0,1},{1,2},{2,3},{3,4},{4,5},{5,6},{6,7},{7,0},{8,9},{9,10},{10,1... | collective-permute-start | bytes 196616 | tf_op jit(solution)/shard_map/ppermute | solution.py:18
  193.8 1.1 collective-permute-start.8
  195.7 1.8 collective-permute-start.9
  197.6 2.3 %collective-permute-start.10 = (bf16[64,512]{1,0:T(8,128)(2,1)S(1)}, bf16[64,512]{1,0:T(8,128)(2,1)S(1)}, u32[]{:S(2)}, u32[]{:S(2)}) collective-permute-start(bf16[64,512]{1,0:T(8,128)(2,1)S(1)} %collective-permute-done.8), channel_id=1, source_target_pairs={{0,7},{1,0},{2,1},{3,2},{4,3},{5,4},{6,5},{7,6},{8,15},{9,8},{10,9... | collective-permute-start | bytes 196616 | tf_op jit(solution)/shard_map/ppermute | solution.py:21
  201.3 3.5 %collective-permute-start.12 = (bf16[64,512]{1,0:T(8,128)(2,1)S(1)}, bf16[64,512]{1,0:T(8,128)(2,1)S(1)}, u32[]{:S(2)}, u32[]{:S(2)}) collective-permute-start(bf16[64,512]{1,0:T(8,128)(2,1)S(1)} %collective-permute-done.10), channel_id=1, source_target_pairs={{0,7},{1,0},{2,1},{3,2},{4,3},{5,4},{6,5},{7,6},{8,15},{9,8},{10,9... | collective-permute-start | bytes 196616 | tf_op jit(solution)/shard_map/ppermute | solution.py:21
  205.7 4.7 %collective-permute-done.13 = bf16[64,512]{1,0:T(8,128)(2,1)S(1)} collective-permute-done((bf16[64,512]{1,0:T(8,128)(2,1)S(1)}, bf16[64,512]{1,0:T(8,128)(2,1)S(1)}, u32[]{:S(2)}, u32[]{:S(2)}) %collective-permute-start.13) | collective-permute-done | bytes 65568 | tf_op jit(solution)/shard_map/ppermute | solution.py:18
  210.4 0.9 fusion.4
  (73 shorter events, 8.4 us)
Async XLA Ops:
  0.0 98.8 %copy-start = (bf16[64,128,128]{2,1,0:T(8,128)(2,1)S(1)}, bf16[64,128,128]{2,1,0:T(8,128)(2,1)}, u32[]{:S(2)}) copy-start(bf16[64,128,128]{2,1,0:T(8,128)(2,1)} %param.14) | copy-start | bytes 6291460
  2.9 24.2 %all-to-all-start = ((s32[64,1,2]{2,1,0:T(1,128)}), s32[64,1,2]{2,1,0:T(1,128)S(1)}, u32[]{:S(2)}, u32[]{:S(2)}) async-start(s32[64,1,2]{2,1,0:T(1,128)} %copy.25), calls=%async_computation | async-start | bytes 65536 | tf_op jit(solution)/shard_map/all_to_all | solution.py:74
  33.8 8.3 %copy-start.5 = (s32[64]{0:T(128)S(1)}, s32[64]{0:T(128)}, u32[]{:S(2)}) copy-start(s32[64]{0:T(128)} %param.16) | copy-start | bytes 772
  33.8 62.7 %all-to-all-start.1 = ((bf16[64,128,128]{2,0,1:T(8,128)(2,1)}), bf16[64,128,128]{2,0,1:T(8,128)(2,1)}, u32[]{:S(2)}, u32[]{:S(2)}) async-start(bf16[64,128,128]{2,0,1:T(8,128)(2,1)} %select_bitcast_fusion.1), calls=%async_computation.1 | async-start | bytes 4194304 | tf_op jit(solution)/shard_map/all_to_all | solution.py:40
  98.8 1.6 copy-start.3
  100.4 19.3 %copy-start.1 = (bf16[64,512]{1,0:T(8,128)(2,1)S(1)}, bf16[64,512]{1,0:T(8,128)(2,1)}, u32[]{:S(2)}) copy-start(bf16[64,512]{1,0:T(8,128)(2,1)} %param.18) | copy-start | bytes 196612
  100.4 19.3 %copy-start.6 = (f32[64]{0:T(128)S(1)}, f32[64]{0:T(128)}, u32[]{:S(2)}) copy-start(f32[64]{0:T(128)} %param.19) | copy-start | bytes 772
  102.4 4.2 %collective-permute-start = (bf16[64,512]{1,0:T(8,128)(2,1)S(1)}, bf16[64,512]{1,0:T(8,128)(2,1)S(1)}, u32[]{:S(2)}, u32[]{:S(2)}) collective-permute-start(bf16[64,512]{1,0:T(8,128)(2,1)S(1)} %bitcast.61), channel_id=1, source_target_pairs={{0,1},{1,2},{2,3},{3,4},{4,5},{5,6},{6,7},{7,0},{8,9},{9,10},{10,1... | collective-permute-start | bytes 196616 | tf_op jit(solution)/shard_map/ppermute | solution.py:18
  105.3 3.7 %collective-permute-start.1 = (bf16[64,512]{1,0:T(8,128)(2,1)S(1)}, bf16[64,512]{1,0:T(8,128)(2,1)S(1)}, u32[]{:S(2)}, u32[]{:S(2)}) collective-permute-start(bf16[64,512]{1,0:T(8,128)(2,1)S(1)} %bitcast.62), channel_id=1, source_target_pairs={{0,7},{1,0},{2,1},{3,2},{4,3},{5,4},{6,5},{7,6},{8,15},{9,8},{10,9... | collective-permute-start | bytes 196616 | tf_op jit(solution)/shard_map/ppermute | solution.py:21
  106.6 3.7 %collective-permute-start.2 = (bf16[64,512]{1,0:T(8,128)(2,1)S(1)}, bf16[64,512]{1,0:T(8,128)(2,1)S(1)}, u32[]{:S(2)}, u32[]{:S(2)}) collective-permute-start(bf16[64,512]{1,0:T(8,128)(2,1)S(1)} %collective-permute-done), channel_id=1, source_target_pairs={{0,1},{1,2},{2,3},{3,4},{4,5},{5,6},{6,7},{7,0},{8,9},{9,10},{10,1... | collective-permute-start | bytes 196616 | tf_op jit(solution)/shard_map/ppermute | solution.py:18
  109.0 4.0 %collective-permute-start.3 = (bf16[64,512]{1,0:T(8,128)(2,1)S(1)}, bf16[64,512]{1,0:T(8,128)(2,1)S(1)}, u32[]{:S(2)}, u32[]{:S(2)}) collective-permute-start(bf16[64,512]{1,0:T(8,128)(2,1)S(1)} %collective-permute-done.1), channel_id=1, source_target_pairs={{0,7},{1,0},{2,1},{3,2},{4,3},{5,4},{6,5},{7,6},{8,15},{9,8},{10,9... | collective-permute-start | bytes 196616 | tf_op jit(solution)/shard_map/ppermute | solution.py:21
  110.3 4.4 %collective-permute-start.4 = (bf16[64,512]{1,0:T(8,128)(2,1)S(1)}, bf16[64,512]{1,0:T(8,128)(2,1)S(1)}, u32[]{:S(2)}, u32[]{:S(2)}) collective-permute-start(bf16[64,512]{1,0:T(8,128)(2,1)S(1)} %collective-permute-done.2), channel_id=1, source_target_pairs={{0,1},{1,2},{2,3},{3,4},{4,5},{5,6},{6,7},{7,0},{8,9},{9,10},{10,1... | collective-permute-start | bytes 196616 | tf_op jit(solution)/shard_map/ppermute | solution.py:18
  113.0 3.7 %collective-permute-start.5 = (bf16[64,512]{1,0:T(8,128)(2,1)S(1)}, bf16[64,512]{1,0:T(8,128)(2,1)S(1)}, u32[]{:S(2)}, u32[]{:S(2)}) collective-permute-start(bf16[64,512]{1,0:T(8,128)(2,1)S(1)} %collective-permute-done.3), channel_id=1, source_target_pairs={{0,7},{1,0},{2,1},{3,2},{4,3},{5,4},{6,5},{7,6},{8,15},{9,8},{10,9... | collective-permute-start | bytes 196616 | tf_op jit(solution)/shard_map/ppermute | solution.py:21
  114.8 4.9 %collective-permute-start.6 = (bf16[64,512]{1,0:T(8,128)(2,1)S(1)}, bf16[64,512]{1,0:T(8,128)(2,1)S(1)}, u32[]{:S(2)}, u32[]{:S(2)}) collective-permute-start(bf16[64,512]{1,0:T(8,128)(2,1)S(1)} %collective-permute-done.4), channel_id=1, source_target_pairs={{0,1},{1,2},{2,3},{3,4},{4,5},{5,6},{6,7},{7,0},{8,9},{9,10},{10,1... | collective-permute-start | bytes 196616 | tf_op jit(solution)/shard_map/ppermute | solution.py:18
  187.7 22.7 %copy-start.2 = (bf16[64,512]{1,0:T(8,128)(2,1)S(1)}, bf16[64,512]{1,0:T(8,128)(2,1)}, u32[]{:S(2)}) copy-start(bf16[64,512]{1,0:T(8,128)(2,1)} %param.20) | copy-start | bytes 196612
  187.7 22.7 %copy-start.4 = (f32[64]{0:T(128)S(1)}, f32[64]{0:T(128)}, u32[]{:S(2)}) copy-start(f32[64]{0:T(128)} %param.21) | copy-start | bytes 772
  189.7 6.0 %collective-permute-start.7 = (bf16[64,512]{1,0:T(8,128)(2,1)S(1)}, bf16[64,512]{1,0:T(8,128)(2,1)S(1)}, u32[]{:S(2)}, u32[]{:S(2)}) collective-permute-start(bf16[64,512]{1,0:T(8,128)(2,1)S(1)} %bitcast.59), channel_id=1, source_target_pairs={{0,1},{1,2},{2,3},{3,4},{4,5},{5,6},{6,7},{7,0},{8,9},{9,10},{10,1... | collective-permute-start | bytes 196616 | tf_op jit(solution)/shard_map/ppermute | solution.py:18
  193.8 3.7 %collective-permute-start.8 = (bf16[64,512]{1,0:T(8,128)(2,1)S(1)}, bf16[64,512]{1,0:T(8,128)(2,1)S(1)}, u32[]{:S(2)}, u32[]{:S(2)}) collective-permute-start(bf16[64,512]{1,0:T(8,128)(2,1)S(1)} %bitcast.60), channel_id=1, source_target_pairs={{0,7},{1,0},{2,1},{3,2},{4,3},{5,4},{6,5},{7,6},{8,15},{9,8},{10,9... | collective-permute-start | bytes 196616 | tf_op jit(solution)/shard_map/ppermute | solution.py:21
  195.7 4.9 %collective-permute-start.9 = (bf16[64,512]{1,0:T(8,128)(2,1)S(1)}, bf16[64,512]{1,0:T(8,128)(2,1)S(1)}, u32[]{:S(2)}, u32[]{:S(2)}) collective-permute-start(bf16[64,512]{1,0:T(8,128)(2,1)S(1)} %collective-permute-done.7), channel_id=1, source_target_pairs={{0,1},{1,2},{2,3},{3,4},{4,5},{5,6},{6,7},{7,0},{8,9},{9,10},{10,1... | collective-permute-start | bytes 196616 | tf_op jit(solution)/shard_map/ppermute | solution.py:18
  197.6 3.7 %collective-permute-start.10 = (bf16[64,512]{1,0:T(8,128)(2,1)S(1)}, bf16[64,512]{1,0:T(8,128)(2,1)S(1)}, u32[]{:S(2)}, u32[]{:S(2)}) collective-permute-start(bf16[64,512]{1,0:T(8,128)(2,1)S(1)} %collective-permute-done.8), channel_id=1, source_target_pairs={{0,7},{1,0},{2,1},{3,2},{4,3},{5,4},{6,5},{7,6},{8,15},{9,8},{10,9... | collective-permute-start | bytes 196616 | tf_op jit(solution)/shard_map/ppermute | solution.py:21
  200.6 4.9 %collective-permute-start.11 = (bf16[64,512]{1,0:T(8,128)(2,1)S(1)}, bf16[64,512]{1,0:T(8,128)(2,1)S(1)}, u32[]{:S(2)}, u32[]{:S(2)}) collective-permute-start(bf16[64,512]{1,0:T(8,128)(2,1)S(1)} %collective-permute-done.9), channel_id=1, source_target_pairs={{0,1},{1,2},{2,3},{3,4},{4,5},{5,6},{6,7},{7,0},{8,9},{9,10},{10,1... | collective-permute-start | bytes 196616 | tf_op jit(solution)/shard_map/ppermute | solution.py:18
  201.3 4.4 %collective-permute-start.12 = (bf16[64,512]{1,0:T(8,128)(2,1)S(1)}, bf16[64,512]{1,0:T(8,128)(2,1)S(1)}, u32[]{:S(2)}, u32[]{:S(2)}) collective-permute-start(bf16[64,512]{1,0:T(8,128)(2,1)S(1)} %collective-permute-done.10), channel_id=1, source_target_pairs={{0,7},{1,0},{2,1},{3,2},{4,3},{5,4},{6,5},{7,6},{8,15},{9,8},{10,9... | collective-permute-start | bytes 196616 | tf_op jit(solution)/shard_map/ppermute | solution.py:21
  205.5 4.9 %collective-permute-start.13 = (bf16[64,512]{1,0:T(8,128)(2,1)S(1)}, bf16[64,512]{1,0:T(8,128)(2,1)S(1)}, u32[]{:S(2)}, u32[]{:S(2)}) collective-permute-start(bf16[64,512]{1,0:T(8,128)(2,1)S(1)} %collective-permute-done.11), channel_id=1, source_target_pairs={{0,1},{1,2},{2,3},{3,4},{4,5},{5,6},{6,7},{7,0},{8,9},{9,10},{10,1... | collective-permute-start | bytes 196616 | tf_op jit(solution)/shard_map/ppermute | solution.py:18
